TPU v7x, 256 devices: a whole 4x4x8 slice. The times are simulated.
256 devices in a mesh: block: 8 (over z), tile: 32 (over x, y, core).
Axes of the slice: x: 4, y: 4, z: 8, core: 2. Of those that a mesh axis runs over, the one named last changes fastest.
Arguments:
- acts: bfloat16 [16, 32, 64, 384], P('block', 'tile'), may hold values from -6 to 6
- gamma: float32 [384], replicated, may hold values from 0.25 to 1.75
- beta: float32 [384], replicated, may hold values from -3 to 3
- weights: bfloat16 [384, 27, 192], P('tile'), may hold values from -0.0625 to 0.0625
- cotangent: bfloat16 [16, 64, 128, 192], P('block', 'tile'), may hold values from -6 to 6
Outputs:
- d_acts: bfloat16 [16, 32, 64, 384], P('block', 'tile')
- d_weights: float32 [384, 27, 192], P('tile')
All inputs are finite; a program needn't handle non-finite values.
Results may differ from a plain program's by a relative error of at most 0.0029.
Values may be sent and summed in bfloat16 or wider, within the bound.
A program may use at most 128 MiB of HBM per device.

v0:
```python
import jax
import jax.numpy as jnp
from jax import lax
from jax.sharding import PartitionSpec as P

GROUPS = 32
norm_eps = 1e-06


def from_behind(value, axis, steps):
    count = lax.axis_size(axis)
    first, last = (max(0, -steps), min(count, count - steps))
    return lax.ppermute(value, axis, [(source, source + steps) for source in range(first, last)])


def padded_2(value, sides, width):
    for axis, dim in sides:
        size, length = (lax.axis_size(axis), value.shape[dim])
        up = [(i, (i + 1) % size) for i in range(size - 1)]
        down = [(j, i) for i, j in up]
        last = lax.slice_in_dim(value, length - width, length, axis=dim)
        first = lax.slice_in_dim(value, 0, width, axis=dim)
        before = lax.ppermute(last, axis, up)
        after = lax.ppermute(first, axis, down)
        value = jnp.concatenate([before, value, after], axis=dim)
    return value


def group_totals(values, frames, per_group):
    return jnp.sum(values, axis=(1, 2)).reshape(frames, GROUPS, per_group).sum(-1)


def shards(acts, gamma, beta, weights, cotangent):
    frames, low_rows, low_cols, channels = acts.shape
    tiles = lax.axis_size("tile")
    per_group = channels // GROUPS
    group_size = low_rows * tiles * low_cols * per_group
    acts_wide = acts.astype(jnp.float32)
    stat_sum = group_totals(acts_wide, frames, per_group)
    stat_sq = group_totals(acts_wide * acts_wide, frames, per_group)
    stat_sum, stat_sq = lax.psum((stat_sum, stat_sq), "tile")
    group_mean = stat_sum / group_size
    inv_std = lax.rsqrt(stat_sq / group_size - group_mean * group_mean + norm_eps)
    mean_chan = jnp.repeat(group_mean, per_group, axis=1)[:, None, None, :]
    inv_chan = jnp.repeat(inv_std, per_group, axis=1)[:, None, None, :]
    normed = (acts_wide - mean_chan) * inv_chan
    shifted = normed * gamma + beta
    gate_value = jax.nn.sigmoid(shifted)
    hidden = (shifted * gate_value).astype(jnp.bfloat16)
    previous = from_behind(hidden, "block", 1)
    joined = jnp.concatenate([previous, hidden], 0)
    padded = padded_2(joined, (("tile", 1),), 1)
    upsampled = jnp.repeat(jnp.repeat(padded, 2, axis=1), 2, axis=2)[:, 1 : 2 * low_rows + 3]
    upsampled = jnp.pad(upsampled, ((0, 0), (0, 0), (1, 1), (0, 0)))
    following = from_behind(cotangent, "block", -1)
    grad_field = jnp.concatenate([cotangent, following], 0)
    grad_field = padded_2(grad_field, (("tile", 1),), 1)
    grad_field = jnp.pad(grad_field, ((0, 0), (0, 0), (1, 1), (0, 0)))
    up_rows = 2 * low_rows
    up_cols = 2 * low_cols
    num_cells = frames * up_rows * up_cols
    tap_list = [(tap // 9, tap // 3 % 3, tap % 3) for tap in range(27)]
    windows = [
        grad_field[
            2 - tap_t : 2 - tap_t + frames,
            2 - tap_h : 2 - tap_h + up_rows,
            2 - tap_w : 2 - tap_w + up_cols,
        ].reshape(num_cells, -1)
        for tap_t, tap_h, tap_w in tap_list
    ]
    columns = jnp.concatenate(windows, 1)
    piece_rows = lax.all_gather(weights, "tile", axis=0, tiled=True)
    flat_rows = piece_rows.reshape(piece_rows.shape[0], -1)
    back_grad = lax.dot_general(
        columns, flat_rows, (((1,), (1,)), ((), ())), preferred_element_type=jnp.float32
    )
    back_grad = back_grad.reshape(frames, low_rows, 2, low_cols, 2, piece_rows.shape[0])
    act_grad = back_grad.sum(axis=(2, 4))
    silu_slope = gate_value * (1.0 + shifted * (1.0 - gate_value))
    norm_grad = act_grad * silu_slope * gamma
    first_sum = group_totals(norm_grad, frames, per_group)
    second_sum = group_totals(norm_grad * normed, frames, per_group)
    first_sum, second_sum = lax.psum((first_sum, second_sum), "tile")
    first_chan = jnp.repeat(first_sum / group_size, per_group, axis=1)[:, None, None, :]
    second_chan = jnp.repeat(second_sum / group_size, per_group, axis=1)[:, None, None, :]
    d_acts = (inv_chan * (norm_grad - first_chan - normed * second_chan)).astype(jnp.bfloat16)
    flat_grads = cotangent.reshape(num_cells, -1)
    term_list = []
    for tap_t, tap_h, tap_w in tap_list:
        window_h = upsampled[
            tap_t : tap_t + frames, tap_h : tap_h + up_rows, tap_w : tap_w + up_cols
        ].reshape(num_cells, channels)
        term_list.append(
            lax.dot_general(
                window_h, flat_grads, (((0,), (0,)), ((), ())), preferred_element_type=jnp.float32
            )
        )
    whole_terms = jnp.stack(term_list, 1)
    whole_terms = lax.psum(whole_terms, "block")
    d_weights = lax.psum_scatter(whole_terms, "tile", scatter_dimension=0, tiled=True)
    return (d_acts, d_weights)


def solution(mesh):
    placed = (
        P("block", "tile", None, None),
        P(),
        P(),
        P("tile", None, None),
        P("block", "tile", None, None),
    )
    return jax.shard_map(
        shards,
        mesh=mesh,
        in_specs=placed,
        out_specs=(P("block", "tile", None, None), P("tile", None, None)),
        check_vma=False,
    )
```

profile of v0, /device:TPU:2, one launch (start us, length us, event | category | flops | bytes accessed | tf_op | source)
XLA Modules:
  0.0 430.7 jit_solution(1480891718286037013)
XLA Ops:
  7.9 1.3 collective-permute-start
  9.2 1.1 copy.87
  11.7 56.1 %all-reduce.3 = (f32[2,32]{1,0:T(2,128)S(1)}, f32[2,32]{1,0:T(2,128)S(1)}) all-reduce(f32[2,32]{1,0:T(2,128)S(1)} %reduce_sum.86, f32[2,32]{1,0:T(2,128)S(1)} %reduce_sum.84), channel_id=1, replica_groups=mesh['block'=8,'tile'=32] {'tile'}, use_global_device_ids=true, to_apply=%region_5.0 | all-reduce | flops 128 | bytes 1024 | tf_op jit(solution)/shard_map/psum | solution.py:41
  68.8 1.9 collective-permute-start.1
  70.8 5.8 %collective-permute-start.2 = (bf16[4,1,128,192]{2,3,1,0:T(8,128)(2,1)S(1)}, bf16[4,1,128,192]{2,3,1,0:T(8,128)(2,1)S(1)}, u32[]{:S(2)}, u32[]{:S(2)}) collective-permute-start(bf16[4,1,128,192]{2,3,1,0:T(8,128)(2,1)S(1)} %get-tuple-element.44), channel_id=1, source_target_pairs={{1,0},{2,1},{3,2},{4,3},{5,4},{6,5},{7,6},{8,7},{9,8},{10,9},{11,1... | collective-permute-start | bytes 589832 | tf_op jit(solution)/shard_map/ppermute | solution.py:24
  77.9 1.8 collective-permute-done.2
  81.9 1.1 copy.78
  83.8 2.5 fusion.110
  86.9 1.1 copy.88
  88.0 1.8 copy.86
  90.8 1.8 copy.85
  92.6 1.7 copy.112
  94.3 1.8 copy.83
  96.1 1.7 copy.110
  97.7 1.8 copy.82
  99.5 1.7 copy.109
  101.2 1.8 copy.80
  103.0 1.7 copy.107
  104.7 1.8 copy.79
  106.5 1.7 copy.106
  108.2 1.8 copy.77
  110.0 1.7 copy.104
  111.7 1.8 copy.76
  113.5 1.7 copy.103
  115.2 1.8 copy.74
  117.0 1.7 copy.101
  118.7 1.8 copy.73
  120.5 1.7 copy.100
  122.1 1.8 copy.71
  123.9 1.7 copy.98
  125.6 1.8 copy.70
  127.4 1.7 copy.97
  129.1 1.8 copy.68
  130.9 1.7 copy.95
  132.5 1.8 copy.67
  134.3 1.7 copy.94
  136.0 1.8 copy.65
  137.8 1.7 copy.92
  139.5 9.7 %concatenate.111 = bf16[2,1,2,64,2,5184]{5,3,4,2,0,1:T(8,128)(2,1)} concatenate(bf16[2,1,2,64,2,192]{5,3,4,2,0,1:T(8,128)(2,1)} %copy.92, bf16[2,1,2,64,2,192]{5,3,4,2,0,1:T(8,128)(2,1)S(1)} %copy.93, bf16[2,1,2,64,2,192]{5,3,4,2,0,1:T(8,128)(2,1)} %copy.94, bf16[2,1,2,64,2,192]{5,3,4,2,0,1:T(8,128)(2,1)} %copy.95, bf16[2,1,2,64,2,192]{5,3,4,2,0,1:T(8,128)(2,1)S(1)} %copy.96, ...), dimensions={5} | concatenate | bytes 10616832 | tf_op jit(solution)/shard_map/concatenate | solution.py:71
  149.2 8.6 %copy.119 = bf16[384,27,192]{0,2,1:T(8,128)(2,1)} copy(bf16[384,27,192]{2,1,0:T(8,128)(2,1)} %all-gather.2.cloned.1.call-done) | data formatting | bytes 7962624 | tf_op jit(solution)/shard_map/all_gather | solution.py:72
  157.8 6.7 %fusion.8 = f32[2,64,384]{2,1,0:T(8,128)S(1)} fusion(bf16[384,5184,1,1,1]{0,1,4,3,2:T(8,128)(2,1)} %bitcast.286, bf16[2,1,2,64,2,5184]{5,3,4,2,0,1:T(8,128)(2,1)} %concatenate.111), kind=kOutput, calls=%fused_computation.10 | convolution fusion | flops 2038579200 | bytes 9486336 | tf_op jit(solution)/shard_map/dot_general | solution.py:74
  164.7 4.4 %collective-permute-start.3 = (bf16[2,1,64,384]{3,2,1,0:T(8,128)(2,1)S(1)}, bf16[2,1,64,384]{3,2,1,0:T(8,128)(2,1)S(1)}, u32[]{:S(2)}, u32[]{:S(2)}) collective-permute-start(bf16[2,1,64,384]{3,2,1,0:T(8,128)(2,1)S(1)} %get-tuple-element.45), channel_id=1, source_target_pairs={{0,32},{32,64},{64,96},{96,128},{128,160},{160,192},{192,224},{1,3... | collective-permute-start | bytes 294920 | tf_op jit(solution)/shard_map/ppermute | solution.py:13
  169.1 2.2 collective-permute-done.3
  171.3 5.1 %collective-permute-start.5 = (bf16[4,1,64,384]{3,2,1,0:T(8,128)(2,1)S(1)}, bf16[4,1,64,384]{3,2,1,0:T(8,128)(2,1)S(1)}, u32[]{:S(2)}, u32[]{:S(2)}) collective-permute-start(bf16[4,1,64,384]{3,2,1,0:T(8,128)(2,1)S(1)} %pad_maximum_fusion.3), channel_id=1, source_target_pairs={{1,0},{2,1},{3,2},{4,3},{5,4},{6,5},{7,6},{8,7},{9,8},{10,9},{11,1... | collective-permute-start | bytes 589832 | tf_op jit(solution)/shard_map/ppermute | solution.py:24
  176.4 2.1 collective-permute-start.4
  178.5 1.1 collective-permute-done.5
  179.5 5.9 %collective-permute-done.4 = bf16[4,1,64,384]{3,2,1,0:T(8,128)(2,1)S(1)} collective-permute-done((bf16[4,1,64,384]{3,2,1,0:T(8,128)(2,1)S(1)}, bf16[4,1,64,384]{3,2,1,0:T(8,128)(2,1)S(1)}, u32[]{:S(2)}, u32[]{:S(2)}) %collective-permute-start.4) | collective-permute-done | bytes 196640 | tf_op jit(solution)/shard_map/ppermute | solution.py:23
  185.7 3.2 broadcast_in_dim.26
  188.9 5.1 %reshape.166 = bf16[4,6,128,384]{3,2,1,0:T(8,128)(2,1)S(1)} reshape(bf16[4,6,64,2,384]{4,3,2,1,0:T(2,128)(2,1)} %broadcast_in_dim.26) | data formatting | bytes 4718592 | tf_op jit(solution)/shard_map/reshape | solution.py:53
  194.2 1.0 fusion.37
  196.2 1.0 fusion.35
  197.2 1.0 fusion.34
  199.2 1.0 fusion.32
  200.2 1.0 fusion.31
  202.2 1.0 fusion.29
  203.2 1.0 fusion.28
  205.2 1.0 fusion.26
  217.0 1.0 fusion.14
  218.0 1.0 fusion.13
  220.9 12.0 %copy.120 = f32[384,27,192]{2,1,0:T(8,128)} copy(f32[384,27,192]{0,2,1:T(8,128)} %fusion.11) | data formatting | bytes 15925248 | tf_op jit(solution)/shard_map/stack | solution.py:98
  233.4 53.0 %all-reduce.2 = (f32[2,32]{1,0:T(2,128)S(1)}, f32[2,32]{1,0:T(2,128)S(1)}) all-reduce(f32[2,32]{1,0:T(2,128)S(1)} %reduce_sum.92, f32[2,32]{1,0:T(2,128)S(1)} %reduce_sum.90), channel_id=1, replica_groups=mesh['block'=8,'tile'=32] {'tile'}, use_global_device_ids=true, to_apply=%region_12.13 | all-reduce | flops 128 | bytes 1024 | tf_op jit(solution)/shard_map/psum | solution.py:83
  286.4 60.6 %reduce-scatter.2.cloned.1.call-done = f32[12,27,192]{2,1,0:T(8,128)} async-done(((f32[384,27,192]{2,1,0:T(8,128)}), f32[12,27,192]{2,1,0:T(8,128)}) %reduce-scatter.2.cloned.1.call-update) | async-done | bytes 248848 | tf_op jit(solution)/shard_map/reduce_scatter | solution.py:100
  348.1 74.3 %all-reduce.6.cloned.1.call-done = f32[12,27,192]{2,1,0:T(8,128)} async-done(((f32[12,27,192]{2,1,0:T(8,128)}), f32[12,27,192]{2,1,0:T(8,128)}) %all-reduce.6.cloned.1.call-update) | async-done | bytes 248848 | tf_op jit(solution)/shard_map/psum | solution.py:99
  422.4 1.8 copy.177
  (86 shorter events, 27.7 us)
Async XLA Ops:
  7.2 142.0 %all-gather.2.cloned.1.call-start = ((), (), s32[]{:S(2)}) async-start(), calls=%async_computation.1 | async-start | bytes 6488064 | tf_op jit(solution)/shard_map/all_gather | solution.py:72
  7.9 339.1 %reduce-scatter.2.cloned.1.call-start = ((), (), s32[]{:S(2)}) async-start(), calls=%async_computation.2 | async-start | bytes 12976128 | tf_op jit(solution)/shard_map/reduce_scatter | solution.py:100
  7.9 60.8 %collective-permute-start = (bf16[2,2,128,192]{2,3,1,0:T(8,128)(2,1)}, bf16[2,2,128,192]{2,3,1,0:T(8,128)(2,1)S(1)}, u32[]{:S(2)}, u32[]{:S(2)}) collective-permute-start(bf16[2,2,128,192]{2,3,1,0:T(8,128)(2,1)} %param.9), channel_id=1, source_target_pairs={{32,0},{64,32},{96,64},{128,96},{160,128},{192,160},{224,192},{33,... | collective-permute-start | bytes 589832 | tf_op jit(solution)/shard_map/ppermute | solution.py:13
  68.8 9.1 %collective-permute-start.1 = (bf16[4,1,128,192]{2,3,1,0:T(8,128)(2,1)S(1)}, bf16[4,1,128,192]{2,3,1,0:T(8,128)(2,1)S(1)}, u32[]{:S(2)}, u32[]{:S(2)}) collective-permute-start(bf16[4,1,128,192]{2,3,1,0:T(8,128)(2,1)S(1)} %get-tuple-element.43), channel_id=1, source_target_pairs={{0,1},{1,2},{2,3},{3,4},{4,5},{5,6},{6,7},{7,8},{8,9},{9,10},{10,1... | collective-permute-start | bytes 589832 | tf_op jit(solution)/shard_map/ppermute | solution.py:23
  70.8 8.9 %collective-permute-start.2 = (bf16[4,1,128,192]{2,3,1,0:T(8,128)(2,1)S(1)}, bf16[4,1,128,192]{2,3,1,0:T(8,128)(2,1)S(1)}, u32[]{:S(2)}, u32[]{:S(2)}) collective-permute-start(bf16[4,1,128,192]{2,3,1,0:T(8,128)(2,1)S(1)} %get-tuple-element.44), channel_id=1, source_target_pairs={{1,0},{2,1},{3,2},{4,3},{5,4},{6,5},{7,6},{8,7},{9,8},{10,9},{11,1... | collective-permute-start | bytes 589832 | tf_op jit(solution)/shard_map/ppermute | solution.py:24
  157.7 6.7 %copy-start.1 = (bf16[2,1,64,384]{3,2,1,0:T(8,128)(2,1)S(1)}, bf16[2,1,64,384]{3,2,1,0:T(8,128)(2,1)}, u32[]{:S(2)}) copy-start(bf16[2,1,64,384]{3,2,1,0:T(8,128)(2,1)} %param.5) | copy-start | bytes 294916
  157.7 6.7 %copy-start.2 = (f32[384]{0:T(512)S(1)}, f32[384]{0:T(512)}, u32[]{:S(2)}) copy-start(f32[384]{0:T(512)} %param.7) | copy-start | bytes 4612
  157.8 6.7 %copy-start.3 = (f32[384]{0:T(512)S(1)}, f32[384]{0:T(512)}, u32[]{:S(2)}) copy-start(f32[384]{0:T(512)} %param.6) | copy-start | bytes 4612
  164.7 6.6 %collective-permute-start.3 = (bf16[2,1,64,384]{3,2,1,0:T(8,128)(2,1)S(1)}, bf16[2,1,64,384]{3,2,1,0:T(8,128)(2,1)S(1)}, u32[]{:S(2)}, u32[]{:S(2)}) collective-permute-start(bf16[2,1,64,384]{3,2,1,0:T(8,128)(2,1)S(1)} %get-tuple-element.45), channel_id=1, source_target_pairs={{0,32},{32,64},{64,96},{96,128},{128,160},{160,192},{192,224},{1,3... | collective-permute-start | bytes 294920 | tf_op jit(solution)/shard_map/ppermute | solution.py:13
  171.3 8.2 %collective-permute-start.5 = (bf16[4,1,64,384]{3,2,1,0:T(8,128)(2,1)S(1)}, bf16[4,1,64,384]{3,2,1,0:T(8,128)(2,1)S(1)}, u32[]{:S(2)}, u32[]{:S(2)}) collective-permute-start(bf16[4,1,64,384]{3,2,1,0:T(8,128)(2,1)S(1)} %pad_maximum_fusion.3), channel_id=1, source_target_pairs={{1,0},{2,1},{3,2},{4,3},{5,4},{6,5},{7,6},{8,7},{9,8},{10,9},{11,1... | collective-permute-start | bytes 589832 | tf_op jit(solution)/shard_map/ppermute | solution.py:24
  176.4 9.1 %collective-permute-start.4 = (bf16[4,1,64,384]{3,2,1,0:T(8,128)(2,1)S(1)}, bf16[4,1,64,384]{3,2,1,0:T(8,128)(2,1)S(1)}, u32[]{:S(2)}, u32[]{:S(2)}) collective-permute-start(bf16[4,1,64,384]{3,2,1,0:T(8,128)(2,1)S(1)} %pad_maximum_fusion.3), channel_id=1, source_target_pairs={{0,1},{1,2},{2,3},{3,4},{4,5},{5,6},{6,7},{7,8},{8,9},{9,10},{10,1... | collective-permute-start | bytes 589832 | tf_op jit(solution)/shard_map/ppermute | solution.py:23
  188.9 5.3 %copy-start = (bf16[2,2,128,192]{2,3,1,0:T(8,128)(2,1)S(1)}, bf16[2,2,128,192]{2,3,1,0:T(8,128)(2,1)}, u32[]{:S(2)}) copy-start(bf16[2,2,128,192]{2,3,1,0:T(8,128)(2,1)} %param.9) | copy-start | bytes 589828
  232.9 189.4 %all-reduce.6.cloned.1.call-start = ((), (), s32[]{:S(2)}) async-start(), calls=%async_computation.3 | async-start | bytes 786432 | tf_op jit(solution)/shard_map/psum | solution.py:99
Sparse Core Ops, SparseCore 0:
  10.5 56.0 all-gather.1
  233.1 113.8 reduce-scatter.1
  349.3 72.9 all-reduce.5
where the time goes:
time: 433 us; the launch traced here: 431 us
  waiting for transfers between devices  147 us (34%)
  blocking collectives  109 us (25%)
  local copies, waits for them, and re-layouts  102 us (24%)
  matrix products  33.4 us (8%)
  starting transfers between devices  20.7 us (5%)
  between operations  14.2 us (3%)
    psum x1, waiting for transfers between devices, shards(): whole_terms = lax.psum(whole_terms, 'block')  74.3 us
    reduce_scatter x1, waiting for transfers between devices, shards(): lax.psum_scatter(whole_terms, 'tile', scatter_dimension=0, tiled=True)  60.6 us
    psum x1, blocking collectives, shards(): stat_sum, stat_sq = lax.psum((stat_sum, stat_sq), 'tile')  56.1 us
    psum x1, blocking collectives, shards(): first_sum, second_sum = lax.psum((first_sum, second_sum), 'tile')  53 us
    concatenate x28, local copies, waits for them, and re-layouts, shards(): columns = jnp.concatenate(windows, 1)  34.5 us
    slice x26, local copies, waits for them, and re-layouts, shards(): grad_field[2 - tap_t:2 - tap_t + frames, 2 - tap_h:2 - tap_h + up_rows, 2...  33.3 us
    dot_general x27, matrix products, shards(): lax.dot_general(window_h, flat_grads, (((0,), (0,)), ((), ())), preferred...  26.7 us
    another operation x1, local copies, waits for them, and re-layouts, shards(): whole_terms = jnp.stack(term_list, 1)  12 us
  transfers between devices with their start and end apart: 9, of which 7 were waited for; matrix products, arithmetic and copies ran while one was open for 17% of the time, Pallas kernels for 0%

commit v1 on v0

--- a/solution.py
+++ b/solution.py
@@ -96,7 +96,7 @@
             )
         )
     whole_terms = jnp.stack(term_list, 1)
-    whole_terms = lax.psum(whole_terms, "block")
+    whole_terms = jnp.sum(lax.all_gather(whole_terms, "block"), axis=0)
     d_weights = lax.psum_scatter(whole_terms, "tile", scatter_dimension=0, tiled=True)
     return (d_acts, d_weights)
 

time: 433 us -> 1050 us (2.42)
  waiting for transfers between devices: 147 us -> 681 us
  local copies, waits for them, and re-layouts: 102 us -> 143 us
  other arithmetic: 3.85 us -> 39.7 us
    all_gather x0 -> x1, waiting for transfers between devices: none -> 615 us  [shards(): whole_terms = jnp.sum(lax.all_gather(whole_terms, 'block'), axis=0)]
    psum x1 -> x0, waiting for transfers between devices: 74.3 us -> none  [shards(): whole_terms = lax.psum(whole_terms, 'block')]
    unnamed x11, local copies, waits for them, and re-layouts: 3.83 us -> 45.2 us
    reduce_sum x0 -> x1, other arithmetic: none -> 35.9 us  [shards(): whole_terms = jnp.sum(lax.all_gather(whole_terms, 'block'), axis=0)]
    another operation x1 -> x0, local copies, waits for them, and re-layouts: 12 us -> none  [shards(): whole_terms = jnp.stack(term_list, 1)]
    reduce_sum x0 -> x1, local copies, waits for them, and re-layouts: none -> 12 us  [shards(): whole_terms = jnp.sum(lax.all_gather(whole_terms, 'block'), axis=0)]
  transfers between devices with their start and end apart: 9 -> 9, of which waited for: 7 -> 7; matrix products, arithmetic and copies ran while one was open for 17% -> 7% of each run, Pallas kernels for 0% -> 0%
where the time goes in v1:
time: 1050 us; the launch traced here: 1040 us
  waiting for transfers between devices  681 us (65%)
  local copies, waits for them, and re-layouts  143 us (14%)
  blocking collectives  111 us (11%)
  other arithmetic  39.7 us (4%)
  matrix products  33.5 us (3%)
  starting transfers between devices  20.9 us (2%)
  between operations  14.2 us (1%)
    all_gather x1, waiting for transfers between devices, shards(): whole_terms = jnp.sum(lax.all_gather(whole_terms, 'block'), axis=0)  615 us
    psum x1, blocking collectives, shards(): stat_sum, stat_sq = lax.psum((stat_sum, stat_sq), 'tile')  56.1 us
    psum x1, blocking collectives, shards(): first_sum, second_sum = lax.psum((first_sum, second_sum), 'tile')  55 us
    reduce_scatter x1, waiting for transfers between devices, shards(): lax.psum_scatter(whole_terms, 'tile', scatter_dimension=0, tiled=True)  53.7 us
    unnamed x11, local copies, waits for them, and re-layouts  45.2 us
    reduce_sum x1, other arithmetic, shards(): whole_terms = jnp.sum(lax.all_gather(whole_terms, 'block'), axis=0)  35.9 us
    concatenate x28, local copies, waits for them, and re-layouts, shards(): columns = jnp.concatenate(windows, 1)  34.5 us
    slice x26, local copies, waits for them, and re-layouts, shards(): grad_field[2 - tap_t:2 - tap_t + frames, 2 - tap_h:2 - tap_h + up_rows, 2...  33.3 us
  transfers between devices with their start and end apart: 9, of which 7 were waited for; matrix products, arithmetic and copies ran while one was open for 7% of the time, Pallas kernels for 0%

profile of v1, /device:TPU:2, one launch (start us, length us, event | category | flops | bytes accessed | tf_op | source)
XLA Modules:
  0.0 1043.9 jit_solution(15683295171595610901)
XLA Ops:
  7.9 1.3 collective-permute-start
  9.2 1.1 copy.141
  11.7 56.1 %all-reduce.3 = (f32[2,32]{1,0:T(2,128)S(1)}, f32[2,32]{1,0:T(2,128)S(1)}) all-reduce(f32[2,32]{1,0:T(2,128)S(1)} %reduce_sum.95, f32[2,32]{1,0:T(2,128)S(1)} %reduce_sum.93), channel_id=1, replica_groups=mesh['block'=8,'tile'=32] {'tile'}, use_global_device_ids=true, to_apply=%region_5.0 | all-reduce | flops 128 | bytes 1024 | tf_op jit(solution)/shard_map/psum | solution.py:41
  68.8 1.9 collective-permute-start.1
  70.8 5.8 collective-permute-start.2
  77.9 1.8 collective-permute-done.2
  81.9 1.1 copy.132
  83.8 2.5 fusion.110
  86.9 1.1 copy.142
  88.0 1.8 copy.140
  90.8 1.8 copy.139
  92.6 1.7 copy.166
  94.3 1.8 copy.137
  96.1 1.7 copy.164
  97.7 1.8 copy.136
  99.5 1.7 copy.163
  101.2 1.8 copy.134
  103.0 1.7 copy.161
  104.7 1.8 copy.133
  106.5 1.7 copy.160
  108.2 1.8 copy.131
  110.0 1.7 copy.158
  111.7 1.8 copy.130
  113.5 1.7 copy.157
  115.2 1.8 copy.128
  117.0 1.7 copy.155
  118.7 1.8 copy.127
  120.5 1.7 copy.154
  122.1 1.8 copy.125
  123.9 1.7 copy.152
  125.6 1.8 copy.124
  127.4 1.7 copy.151
  129.1 1.8 copy.122
  130.9 1.7 copy.149
  132.5 1.8 copy.121
  134.3 1.7 copy.148
  136.0 1.8 copy.119
  137.8 1.7 copy.146
  139.5 9.7 concatenate.111
  149.2 8.6 copy.173
  157.8 6.7 fusion.8
  164.7 4.4 collective-permute-start.3
  169.1 2.2 collective-permute-done.3
  171.3 5.1 collective-permute-start.5
  176.4 2.1 collective-permute-start.4
  178.5 1.1 collective-permute-done.5
  179.5 5.9 collective-permute-done.4
  185.7 3.2 broadcast_in_dim.26
  188.9 5.1 reshape.166
  194.2 1.0 fusion.37
  196.2 1.0 fusion.35
  199.1 1.0 fusion.32
  203.2 1.0 fusion.28
  205.1 1.0 fusion.26
  208.1 1.0 fusion.23
  211.1 1.0 fusion.20
  214.1 1.0 fusion.17
  215.1 1.0 fusion.16
  221.3 615.0 %all-gather.6.cloned.1.call-done = f32[3072,27,192]{0,2,1:T(8,128)} async-done(((f32[384,27,192]{0,2,1:T(8,128)}), f32[3072,27,192]{0,2,1:T(8,128)}) %all-gather.6.cloned.1.call-update) | async-done | bytes 63701008 | tf_op jit(solution)/shard_map/all_gather | solution.py:99
  836.3 43.1 %copy.203 = f32[648,8,8,384]{3,2,1,0:T(8,128)} copy(f32[648,8,8,384]{3,1,2,0:T(8,128)} %bitcast.292) | data formatting | bytes 127401984
  879.4 35.9 %reduce_sum.102 = f32[384,27,192]{0,2,1:T(8,128)} reduce(f32[8,384,27,192]{1,0,3,2:T(8,128)} %bitcast.291, f32[]{:T(128)} %constant.10.clone.1), dimensions={0}, to_apply=%region_13.14 | reduce | flops 13934592 | bytes 71663616 | tf_op jit(solution)/shard_map/reduce_sum | solution.py:99
  915.2 12.0 %copy.174 = f32[384,27,192]{2,1,0:T(8,128)} copy(f32[384,27,192]{0,2,1:T(8,128)} %reduce_sum.102) | data formatting | bytes 15925248 | tf_op jit(solution)/shard_map/reduce_sum | solution.py:99
  927.6 55.0 %all-reduce.2 = (f32[2,32]{1,0:T(2,128)S(1)}, f32[2,32]{1,0:T(2,128)S(1)}) all-reduce(f32[2,32]{1,0:T(2,128)S(1)} %reduce_sum.101, f32[2,32]{1,0:T(2,128)S(1)} %reduce_sum.99), channel_id=1, replica_groups=mesh['block'=8,'tile'=32] {'tile'}, use_global_device_ids=true, to_apply=%region_12.13 | all-reduce | flops 128 | bytes 1024 | tf_op jit(solution)/shard_map/psum | solution.py:83
  983.7 53.7 %reduce-scatter.2.cloned.1.call-done = f32[12,27,192]{2,1,0:T(8,128)} async-done(((f32[384,27,192]{2,1,0:T(8,128)}), f32[12,27,192]{2,1,0:T(8,128)}) %reduce-scatter.2.cloned.1.call-update) | async-done | bytes 248848 | tf_op jit(solution)/shard_map/reduce_scatter | solution.py:100
  (87 shorter events, 29.0 us)
Async XLA Ops:
  7.2 142.0 %all-gather.4.cloned.1.call-start = ((), (), s32[]{:S(2)}) async-start(), calls=%async_computation.1 | async-start | bytes 6488064 | tf_op jit(solution)/shard_map/all_gather | solution.py:72
  7.9 828.4 %all-gather.6.cloned.1.call-start = ((), (), s32[]{:S(2)}) async-start(), calls=%async_computation.3 | async-start | bytes 71663616 | tf_op jit(solution)/shard_map/all_gather | solution.py:99
  7.9 60.8 %collective-permute-start = (bf16[2,2,128,192]{2,3,1,0:T(8,128)(2,1)}, bf16[2,2,128,192]{2,3,1,0:T(8,128)(2,1)S(1)}, u32[]{:S(2)}, u32[]{:S(2)}) collective-permute-start(bf16[2,2,128,192]{2,3,1,0:T(8,128)(2,1)} %param.9), channel_id=1, source_target_pairs={{32,0},{64,32},{96,64},{128,96},{160,128},{192,160},{224,192},{33,... | collective-permute-start | bytes 589832 | tf_op jit(solution)/shard_map/ppermute | solution.py:13
  68.8 9.1 collective-permute-start.1
  70.8 8.9 collective-permute-start.2
  157.7 6.7 copy-start.1
  157.7 6.7 copy-start.2
  157.8 6.7 copy-start.3
  164.7 6.6 collective-permute-start.3
  171.3 8.2 collective-permute-start.5
  176.4 9.1 collective-permute-start.4
  188.9 5.3 copy-start
  221.0 816.4 %reduce-scatter.2.cloned.1.call-start = ((), (), s32[]{:S(2)}) async-start(), calls=%async_computation.2 | async-start | bytes 12976128 | tf_op jit(solution)/shard_map/reduce_scatter | solution.py:100
Sparse Core Ops, SparseCore 0:
  10.5 56.0 all-gather.3
  221.1 615.1 all-gather.5
  927.3 110.0 reduce-scatter.1
